TPU v7x, 32 devices: a whole 2x2x4 slice. The times are simulated.
32 devices in a mesh: row: 8 (over y, x, core), col: 4 (over z).
Axes of the slice: x: 2, y: 2, z: 4, core: 2. Of those that a mesh axis runs over, the one named last changes fastest.
Arguments:
- inverse_blocks: float32 [4096, 4096], P('row', 'col'), may hold values from -0.09375 to 0.09375
- panel: bfloat16 [4096, 4096], P('row', 'col'), may hold values from -1.5 to 1.5
- diag_inverse: float32 [512, 4096], P('row', 'col'), may hold values from -6 to 6
- members: int32 [8, 8], replicated, may hold values from 0 to 7, each once within a row
- counts: int32 [8], replicated, may hold values from 1 to 8, as said below
Outputs:
- offdiag: float32 [4096, 4096], P('row', 'col')
- new_diag: float32 [512, 4096], P('row', 'col')
Inputs may be any that keep to these rules, and one draw needn't show every extreme that they name: Each row of members names every ancestor once. `counts`: some supernode lists all 8 ancestors and some lists one.
All inputs are finite; a program needn't handle non-finite values.
Results may differ from a plain program's by a relative error of at most 0.0003.
Values may be sent and summed in bfloat16 or wider, within the bound.
A program may use at most 128 MiB of HBM per device.

v0:
```python
import jax
import jax.numpy as jnp
from jax import lax
from jax.sharding import PartitionSpec as P

B = 512


def body(inverse_blocks, panel, diag_inverse, members, counts):
    rows_dev = panel.shape[0]
    sup_count = panel.shape[1] // B
    row_index = lax.axis_index("row")
    col_index = lax.axis_index("col")
    ancestor = row_index * rows_dev // B
    first_sup = col_index * sup_count
    local_members = lax.dynamic_slice_in_dim(members, first_sup, sup_count, 0)
    local_counts = lax.dynamic_slice_in_dim(counts, first_sup, sup_count, 0)
    slot_index = jnp.arange(members.shape[1], dtype=jnp.int32)
    live_slot = slot_index[None, :] < local_counts[:, None]
    row_mask = jnp.sum(
        jnp.where((local_members == ancestor) & live_slot, 1.0, 0.0).astype(jnp.float32), axis=1
    )
    column_mask = jnp.repeat(row_mask, B)
    masked = panel * column_mask.astype(jnp.bfloat16)[None, :]
    inverse_rows = lax.all_gather(inverse_blocks, "col", axis=1, tiled=True)
    running = jnp.dot(
        inverse_rows,
        lax.all_gather(masked, "row", axis=0, tiled=True).astype(jnp.float32),
        precision=lax.Precision.HIGHEST,
    )
    offdiag = -(running * column_mask[None, :])
    masked_wide = masked.astype(jnp.float32).reshape(rows_dev, sup_count, B)
    offdiag_wide = offdiag.reshape(rows_dev, sup_count, B)
    diag_terms = jnp.einsum(
        "ikc,ikd->ckd", masked_wide, offdiag_wide, precision=lax.Precision.HIGHEST
    )
    summed = lax.psum_scatter(
        diag_terms.reshape(B, sup_count * B), "row", scatter_dimension=0, tiled=True
    )
    return (offdiag, diag_inverse - summed)


def solution(mesh):
    return jax.shard_map(
        body,
        mesh=mesh,
        in_specs=(P("row", "col"), P("row", "col"), P("row", "col"), P(), P()),
        out_specs=(P("row", "col"), P("row", "col")),
        check_vma=False,
    )
```

profile of v0, /device:TPU:0, one launch (start us, length us, event | category | flops | bytes accessed | tf_op | source)
XLA Modules:
  0.0 291.6 jit_solution(4853133798508175931)
XLA Ops:
  7.2 0.0 copy-start.3
  7.2 0.0 copy-start.1
  7.2 0.0 all-gather.5.cloned.1.call-start
  7.2 0.7 all-gather.5.cloned.1.call-update
  7.9 0.0 all-gather.3.cloned.1.call-start
  8.0 0.0 copy-done.3
  8.0 0.1 dynamic_slice.7
  8.1 0.9 fusion.3
  8.9 0.1 broadcast_bitcast_fusion
  9.0 0.0 copy-done.1
  9.0 1.0 broadcast_multiply_fusion
  10.1 0.0 all-gather.3.cloned.1.call-update
  10.1 0.0 copy-start
  10.1 0.0 reduce-scatter.2.cloned.1.call-start
  10.2 151.8 %all-gather.5.cloned.1.call-done = f32[512,4096]{1,0:T(8,128)} async-done(((f32[512,1024]{1,0:T(8,128)}), f32[512,4096]{1,0:T(8,128)}) %all-gather.5.cloned.1.call-update) | async-done | bytes 8388624 | tf_op jit(solution)/shard_map/all_gather | solution.py:25
  162.0 55.1 %all-gather.3.cloned.1.call-done = bf16[4096,1024]{1,0:T(8,128)(2,1)} async-done(((bf16[512,1024]{1,0:T(8,128)(2,1)}), bf16[4096,1024]{1,0:T(8,128)(2,1)}) %all-gather.3.cloned.1.call-update) | async-done | bytes 8388624 | tf_op jit(solution)/shard_map/all_gather | solution.py:28
  217.0 18.9 %multiply_negate_fusion = f32[1024,512]{1,0:T(8,128)S(1)} fusion(bf16[4096,1024]{1,0:T(8,128)(2,1)} %all-gather.3.cloned.1.call-done, f32[512,4096]{1,0:T(8,128)} %all-gather.5.cloned.1.call-done, f32[1024]{0:T(1024)S(1)} %bitcast.21), kind=kOutput, calls=%fused_computation | convolution fusion | flops 25770852352 | bytes 18878464 | tf_op jit(solution)/shard_map/dot_general | solution.py:26
  235.9 0.0 copy-done
  235.9 3.1 %fusion = f32[2,512,512]{2,1,0:T(8,128)} fusion(f32[512,2,512]{0,2,1:T(8,128)S(1)} %bitcast.17, bf16[64,2,8,512]{3,2,1,0:T(8,128)(2,1)S(1)} %bitcast.16), kind=kOutput, calls=%fused_computation.1 | convolution fusion | flops 3221225472 | bytes 5242880 | tf_op jit(solution)/shard_map/ikc,ikd->ckd/dot_general | solution.py:34
  239.0 2.9 %copy.8 = f32[512,1024]{1,0:T(8,128)} copy(f32[512,1024]{0,1:T(8,128)} %bitcast.19) | data formatting | bytes 4194304 | tf_op jit(solution)/shard_map/reshape | solution.py:38
  242.0 0.0 reduce-scatter.2.cloned.1.call-update
  242.0 0.0 copy-start.2
  242.0 1.8 copy.9
  243.8 39.6 %reduce-scatter.2.cloned.1.call-done = f32[64,1024]{1,0:T(8,128)} async-done(((f32[512,1024]{1,0:T(8,128)}), f32[64,1024]{1,0:T(8,128)}) %reduce-scatter.2.cloned.1.call-update) | async-done | bytes 262160 | tf_op jit(solution)/shard_map/reduce_scatter | solution.py:37
  283.4 0.0 copy-done.2
  283.4 1.7 sub.8
  (2 shorter events, 0.0 us)
Async XLA Ops:
  7.2 0.8 copy-start.3
  7.2 1.9 copy-start.1
  7.2 154.8 %all-gather.5.cloned.1.call-start = ((), (), s32[]{:S(2)}) async-start(), calls=%async_computation.2 | async-start | bytes 10485760 | tf_op jit(solution)/shard_map/all_gather | solution.py:25
  7.9 209.1 %all-gather.3.cloned.1.call-start = ((), (), s32[]{:S(2)}) async-start(), calls=%async_computation.1 | async-start | bytes 9437184 | tf_op jit(solution)/shard_map/all_gather | solution.py:28
  10.1 225.8 %copy-start = (bf16[512,1024]{1,0:T(8,128)(2,1)S(1)}, bf16[512,1024]{1,0:T(8,128)(2,1)}, u32[]{:S(2)}) copy-start(bf16[512,1024]{1,0:T(8,128)(2,1)} %broadcast_multiply_fusion) | copy-start | bytes 3145732
  10.1 273.3 %reduce-scatter.2.cloned.1.call-start = ((), (), s32[]{:S(2)}) async-start(), calls=%async_computation.3 | async-start | bytes 2359296 | tf_op jit(solution)/shard_map/reduce_scatter | solution.py:37
  242.0 41.4 %copy-start.2 = (f32[64,1024]{1,0:T(8,128)S(1)}, f32[64,1024]{1,0:T(8,128)}, u32[]{:S(2)}) copy-start(f32[64,1024]{1,0:T(8,128)} %param.7) | copy-start | bytes 786436
Sparse Core Ops, SparseCore 0:
  9.6 152.3 all-gather.4
  164.4 52.5 all-gather.2
  242.1 41.2 reduce-scatter.1
where the time goes:
time: 292 us
  waiting for transfers between devices  247 us (85%)
  matrix products  22 us (8%)
  between operations  13.8 us (5%)
  local copies, waits for them, and re-layouts  4.93 us (2%)
  other arithmetic  3.6 us (1%)
    all_gather x1, waiting for transfers between devices, body(): inverse_rows = lax.all_gather(inverse_blocks, 'col', axis=1, tiled=True)  152 us
    all_gather x1, waiting for transfers between devices, body(): lax.all_gather(masked, 'row', axis=0, tiled=True).astype(jnp.float32)  55.1 us
    reduce_scatter x1, waiting for transfers between devices, body(): lax.psum_scatter(diag_terms.reshape(B, sup_count * B), 'row', scatter_dim...  39.6 us
    dot_general x1, matrix products, body(): jnp.dot(inverse_rows, lax.all_gather(masked, 'row', axis=0, tiled=True).a...  18.9 us
  transfers between devices with their start and end apart: 3, of which 3 were waited for; matrix products, arithmetic and copies ran while one was open for 1% of the time, Pallas kernels for 0%

commit v1 on v0

--- a/solution.py
+++ b/solution.py
@@ -22,7 +22,12 @@
     )
     column_mask = jnp.repeat(row_mask, B)
     masked = panel * column_mask.astype(jnp.bfloat16)[None, :]
-    inverse_rows = lax.all_gather(inverse_blocks, "col", axis=1, tiled=True)
+    ring = [inverse_blocks]
+    for hop in range(3):
+        ring.append(lax.ppermute(ring[-1], "col", [(dev, (dev + 1) % 4) for dev in range(4)]))
+    inverse_rows = jnp.roll(
+        jnp.concatenate(ring[::-1], axis=1), (lax.axis_index("col") + 1) * ring[0].shape[1], axis=1
+    )
     running = jnp.dot(
         inverse_rows,
         lax.all_gather(masked, "row", axis=0, tiled=True).astype(jnp.float32),

time: 292 us -> 250 us (0.86)
  waiting for transfers between devices: 247 us -> 184 us
  local copies, waits for them, and re-layouts: 4.93 us -> 24.3 us
  starting transfers between devices: 0.12 us -> 3.16 us
    all_gather x1 -> x0, waiting for transfers between devices: 152 us -> none  [body(): inverse_rows = lax.all_gather(inverse_blocks, 'col', axis=1, tiled=True)]
    ppermute x0 -> x3, waiting for transfers between devices: none -> 145 us  [body(): lax.ppermute(ring[-1], 'col', [(dev, (dev + 1) % 4) for dev in range(4)])]
    all_gather x1, waiting for transfers between devices: 55.1 us -> 0.01 us  [body(): lax.all_gather(masked, 'row', axis=0, tiled=True).astype(jnp.float32)]
    unnamed x11 -> x21, local copies, waits for them, and re-layouts: 1.91 us -> 18.1 us
    ppermute x0 -> x3, starting transfers between devices: none -> 3.08 us  [body(): lax.ppermute(ring[-1], 'col', [(dev, (dev + 1) % 4) for dev in range(4)])]
  transfers between devices with their start and end apart: 3 -> 5, of which waited for: 3 -> 4; matrix products, arithmetic and copies ran while one was open for 1% -> 7% of each run, Pallas kernels for 0% -> 0%
where the time goes in v1:
time: 250 us
  waiting for transfers between devices  184 us (74%)
  local copies, waits for them, and re-layouts  24.3 us (10%)
  matrix products  19.7 us (8%)
  between operations  14.1 us (6%)
  other arithmetic  4.89 us (2%)
  starting transfers between devices  3.16 us (1%)
    ppermute x3, waiting for transfers between devices, body(): lax.ppermute(ring[-1], 'col', [(dev, (dev + 1) % 4) for dev in range(4)])  145 us
    reduce_scatter x1, waiting for transfers between devices, body(): lax.psum_scatter(diag_terms.reshape(B, sup_count * B), 'row', scatter_dim...  39.1 us
    unnamed x21, local copies, waits for them, and re-layouts  18.1 us
    dot_general x1, matrix products, body(): jnp.dot(inverse_rows, lax.all_gather(masked, 'row', axis=0, tiled=True).a...  16.3 us
  transfers between devices with their start and end apart: 5, of which 4 were waited for; matrix products, arithmetic and copies ran while one was open for 7% of the time, Pallas kernels for 0%

profile of v1, /device:TPU:0, one launch (start us, length us, event | category | flops | bytes accessed | tf_op | source)
XLA Modules:
  0.0 249.8 jit_solution(7838764209143432098)
XLA Ops:
  7.2 0.0 copy-start.1
  7.2 0.0 all-gather.2.cloned.1.call-start
  7.2 0.9 dynamic_slice.12
  8.1 0.9 fusion.7
  9.0 0.1 broadcast_bitcast_fusion
  9.1 2.3 broadcast_multiply_fusion
  11.4 0.0 all-gather.2.cloned.1.call-update
  11.4 0.0 reduce-scatter.2.cloned.1.call-start
  11.5 3.1 %collective-permute-start = (f32[512,1024]{1,0:T(8,128)}, f32[512,1024]{1,0:T(8,128)S(1)}, u32[]{:S(2)}, u32[]{:S(2)}) collective-permute-start(f32[512,1024]{1,0:T(8,128)} %param.5), channel_id=1, source_target_pairs={{0,1},{1,2},{2,3},{3,0},{4,5},{5,6},{6,7},{7,4},{8,9},{9,10},{10,1... | collective-permute-start | bytes 6291464 | tf_op jit(solution)/shard_map/ppermute | solution.py:27
  14.6 47.9 %collective-permute-done = f32[512,1024]{1,0:T(8,128)S(1)} collective-permute-done((f32[512,1024]{1,0:T(8,128)}, f32[512,1024]{1,0:T(8,128)S(1)}, u32[]{:S(2)}, u32[]{:S(2)}) %collective-permute-start) | collective-permute-done | bytes 2097184 | tf_op jit(solution)/shard_map/ppermute | solution.py:27
  62.4 1.3 copy-done.2
  63.7 0.0 collective-permute-start.1
  63.7 48.7 %collective-permute-done.1 = f32[512,1024]{1,0:T(8,128)} collective-permute-done((f32[512,1024]{1,0:T(8,128)S(1)}, f32[512,1024]{1,0:T(8,128)}, u32[]{:S(2)}, u32[]{:S(2)}) %collective-permute-start.1) | collective-permute-done | bytes 2097184 | tf_op jit(solution)/shard_map/ppermute | solution.py:27
  112.5 0.0 collective-permute-start.2
  112.5 48.0 %collective-permute-done.2 = f32[512,1024]{1,0:T(8,128)} collective-permute-done((f32[512,1024]{1,0:T(8,128)}, f32[512,1024]{1,0:T(8,128)}, u32[]{:S(2)}, u32[]{:S(2)}) %collective-permute-start.2) | collective-permute-done | bytes 2097184 | tf_op jit(solution)/shard_map/ppermute | solution.py:27
  160.5 3.1 %constant_dynamic-update-slice_fusion.7 = f32[512,8192]{1,0:T(8,128)} fusion(f32[512,1024]{1,0:T(8,128)} %collective-permute-done.2), kind=kLoop, calls=%fused_computation.14 | loop fusion | bytes 4194304
  163.6 3.1 %constant_dynamic-update-slice_fusion.6 = f32[512,8192]{1,0:T(8,128)} fusion(f32[512,8192]{1,0:T(8,128)} %constant_dynamic-update-slice_fusion.7, f32[512,1024]{1,0:T(8,128)} %collective-permute-done.1), kind=kLoop, calls=%fused_computation.13 | loop fusion | bytes 4194304
  166.7 1.4 constant_dynamic-update-slice_fusion.5
  168.1 1.4 constant_dynamic-update-slice_fusion.4
  169.5 3.1 %constant_dynamic-update-slice_fusion.3 = f32[512,8192]{1,0:T(8,128)} fusion(f32[512,8192]{1,0:T(8,128)} %constant_dynamic-update-slice_fusion.4, f32[512,1024]{1,0:T(8,128)} %collective-permute-done.2), kind=kLoop, calls=%fused_computation.10 | loop fusion | bytes 4194304
  172.6 3.1 %constant_dynamic-update-slice_fusion.2 = f32[512,8192]{1,0:T(8,128)} fusion(f32[512,8192]{1,0:T(8,128)} %constant_dynamic-update-slice_fusion.3, f32[512,1024]{1,0:T(8,128)} %collective-permute-done.1), kind=kLoop, calls=%fused_computation.9 | loop fusion | bytes 4194304
  175.8 1.4 constant_dynamic-update-slice_fusion.1
  177.2 1.4 constant_dynamic-update-slice_fusion
  178.6 16.3 %multiply_negate_fusion = f32[512,1024]{1,0:T(8,128)S(1)} fusion(bf16[4096,1024]{1,0:T(8,128)(2,1)} %all-gather.2.cloned.1.call-done, f32[512,8192]{1,0:T(8,128)} %constant_dynamic-update-slice_fusion, s32[]{:T(128)S(6)} %select_n.26, f32[1024]{0:T(1024)S(1)} %bitcast.17), kind=kOutput, calls=%fused_computation.2 | convolution fusion | flops 25770852352 | bytes 18878468 | tf_op jit(solution)/shard_map/dot_general | solution.py:31
  194.9 0.0 copy-start.4
  194.9 0.0 copy-start.5
  194.9 2.0 copy.10
  196.9 3.4 %fusion.4 = f32[2,512,512]{2,1,0:T(8,128)S(1)} fusion(f32[512,2,512]{0,2,1:T(8,128)} %bitcast.15, bf16[64,2,8,512]{3,2,1,0:T(8,128)(2,1)S(1)} %bitcast.13), kind=kOutput, calls=%fused_computation.3 | convolution fusion | flops 3221225472 | bytes 5242880 | tf_op jit(solution)/shard_map/ikc,ikd->ckd/dot_general | solution.py:39
  200.3 1.9 copy.9
  202.2 0.0 reduce-scatter.2.cloned.1.call-update
  202.2 39.1 %reduce-scatter.2.cloned.1.call-done = f32[64,1024]{1,0:T(8,128)} async-done(((f32[512,1024]{1,0:T(8,128)}), f32[64,1024]{1,0:T(8,128)}) %reduce-scatter.2.cloned.1.call-update) | async-done | bytes 262160 | tf_op jit(solution)/shard_map/reduce_scatter | solution.py:42
  241.3 1.7 sub.13
  (11 shorter events, 0.0 us)
Async XLA Ops:
  7.2 160.9 %copy-start.1 = (f32[512,1024]{1,0:T(8,128)S(1)}, f32[512,1024]{1,0:T(8,128)}, u32[]{:S(2)}) copy-start(f32[512,1024]{1,0:T(8,128)} %param.5) | copy-start | bytes 6291460
  7.2 171.4 %all-gather.2.cloned.1.call-start = ((), (), s32[]{:S(2)}) async-start(), calls=%async_computation.1 | async-start | bytes 9437184 | tf_op jit(solution)/shard_map/all_gather | solution.py:33
  11.4 229.9 %reduce-scatter.2.cloned.1.call-start = ((), (), s32[]{:S(2)}) async-start(), calls=%async_computation.2 | async-start | bytes 2359296 | tf_op jit(solution)/shard_map/reduce_scatter | solution.py:42
  11.5 50.9 %collective-permute-start = (f32[512,1024]{1,0:T(8,128)}, f32[512,1024]{1,0:T(8,128)S(1)}, u32[]{:S(2)}, u32[]{:S(2)}) collective-permute-start(f32[512,1024]{1,0:T(8,128)} %param.5), channel_id=1, source_target_pairs={{0,1},{1,2},{2,3},{3,0},{4,5},{5,6},{6,7},{7,4},{8,9},{9,10},{10,1... | collective-permute-start | bytes 6291464 | tf_op jit(solution)/shard_map/ppermute | solution.py:27
  62.4 1.3 copy-start.2
  63.7 48.7 %collective-permute-start.1 = (f32[512,1024]{1,0:T(8,128)S(1)}, f32[512,1024]{1,0:T(8,128)}, u32[]{:S(2)}, u32[]{:S(2)}) collective-permute-start(f32[512,1024]{1,0:T(8,128)S(1)} %collective-permute-done), channel_id=1, source_target_pairs={{0,1},{1,2},{2,3},{3,0},{4,5},{5,6},{6,7},{7,4},{8,9},{9,10},{10,1... | collective-permute-start | bytes 6291464 | tf_op jit(solution)/shard_map/ppermute | solution.py:27
  112.5 48.0 %collective-permute-start.2 = (f32[512,1024]{1,0:T(8,128)}, f32[512,1024]{1,0:T(8,128)}, u32[]{:S(2)}, u32[]{:S(2)}) collective-permute-start(f32[512,1024]{1,0:T(8,128)} %collective-permute-done.1), channel_id=1, source_target_pairs={{0,1},{1,2},{2,3},{3,0},{4,5},{5,6},{6,7},{7,4},{8,9},{9,10},{10,1... | collective-permute-start | bytes 6291464 | tf_op jit(solution)/shard_map/ppermute | solution.py:27
  112.5 54.2 %copy-start.3 = (f32[512,1024]{1,0:T(8,128)S(1)}, f32[512,1024]{1,0:T(8,128)}, u32[]{:S(2)}) copy-start(f32[512,1024]{1,0:T(8,128)} %copy-done.2) | copy-start | bytes 6291460
  178.6 18.4 %copy-start = (bf16[512,1024]{1,0:T(8,128)(2,1)S(1)}, bf16[512,1024]{1,0:T(8,128)(2,1)}, u32[]{:S(2)}) copy-start(bf16[512,1024]{1,0:T(8,128)(2,1)} %broadcast_multiply_fusion) | copy-start | bytes 3145732
  194.9 2.1 copy-start.4
  194.9 46.4 %copy-start.5 = (f32[64,1024]{1,0:T(8,128)S(1)}, f32[64,1024]{1,0:T(8,128)}, u32[]{:S(2)}) copy-start(f32[64,1024]{1,0:T(8,128)} %param.7) | copy-start | bytes 786436
Sparse Core Ops, SparseCore 0:
  11.5 57.0 all-gather.1
  202.3 38.9 reduce-scatter.1
